TPU v7x, 32 devices: a whole 2x2x4 slice. The times are simulated.
32 devices in a mesh: seq: 4 (over z), dp: 8 (over y, x, core).
Axes of the slice: x: 2, y: 2, z: 4, core: 2. Of those that a mesh axis runs over, the one named last changes fastest.
Arguments:
- hidden_in: bfloat16 [16, 2048, 1024], P('dp', 'seq'), may hold values from -6 to 6
- mixer_weights: float32 [1, 5, 1024, 1024], P(None, None, 'dp'), may hold values from -0.1875 to 0.1875
- channel_in_weights: float32 [1, 2, 1024, 2816], P(None, None, 'dp'), may hold values from -0.1875 to 0.1875
- channel_out_weights: float32 [1, 2816, 1024], P(None, 'dp'), may hold values from -0.109375 to 0.109375
- decay_rates: float32 [1, 8], replicated, may hold values from 0 to 0.034, as said below
- doc_lengths: int32 [16, 4], P('dp'), may hold values from 1 to 1024, 2048 in all within a row
- out_cotangent: bfloat16 [16, 2048, 1024], P('dp', 'seq'), may hold values from -6 to 6
Outputs:
- block_output: bfloat16 [16, 2048, 1024], P('dp', 'seq')
- input_gradient: float32 [16, 2048, 1024], P('dp', 'seq')
- mixer_gradient: float32 [1, 5, 1024, 1024], P(None, None, 'dp')
- channel_in_gradient: float32 [1, 2, 1024, 2816], P(None, None, 'dp')
- channel_out_gradient: float32 [1, 2816, 1024], P(None, 'dp')
Inputs may be any that keep to these rules, and one draw needn't show every extreme that they name: `decay_rates`: positive decay rates. `doc_lengths`: each row's 4 lengths add up to 2048.
All inputs are finite; a program needn't handle non-finite values.
Results may differ from a plain program's by a relative error of at most 0.02.
Values may be sent and summed in bfloat16 or wider, within the bound.
No kernel may reach another device: no remote copies, remote signals or barrier semaphores. Data moves between devices by JAX's collectives and lax.ppermute only.
A program may use at most 256 MiB of HBM per device.

v0:
```python
import jax
import jax.numpy as jnp
from jax import lax
from jax.sharding import PartitionSpec as P

EPS = 1e-06
FULL_PRECISION = lax.Precision.HIGHEST


def passed_along(value, axis, steps):
    count = lax.axis_size(axis)
    leading, last = (max(0, -steps), min(count, count - steps))
    return lax.ppermute(value, axis, [(source, source + steps) for source in range(leading, last)])


def product(left, right):
    return jnp.dot(left, right, preferred_element_type=jnp.float32)


def rms_norm(value_rows):
    factor = lax.rsqrt(jnp.mean(value_rows * value_rows, axis=-1, keepdims=True) + EPS)
    return (value_rows * factor, factor)


def norm_back(value_rows, factor, upstream):
    features = value_rows.shape[-1]
    inner_sum = jnp.sum(upstream * value_rows, axis=-1, keepdims=True)
    return factor * upstream - factor * factor * factor / features * value_rows * inner_sum


def swish_slope(value_rows):
    sigmoid_part = jax.nn.sigmoid(value_rows)
    return sigmoid_part * (1.0 + value_rows * (1.0 - sigmoid_part))


def doc_index(doc_ends, places):
    compare = places[None, :, None] >= doc_ends[:, None, :]
    return jnp.sum(compare.astype(jnp.int32), axis=-1, dtype=jnp.int32)


def decay_tables(rates, doc_ends, start, count):
    float_kind = rates.dtype
    offsets = jnp.arange(count, dtype=jnp.int32)
    start = jnp.asarray(start, dtype=jnp.int32)
    doc_here = doc_index(doc_ends, start + offsets)
    before_place = jnp.full((1,), -1, dtype=jnp.int32) + start
    doc_before = doc_index(doc_ends, before_place)[:, 0]
    doc_last = doc_here[:, count - 1]
    distance = jnp.maximum(offsets[:, None] - offsets[None, :], 0).astype(float_kind)
    causal = offsets[:, None] >= offsets[None, :]
    linked = causal[None] & (doc_here[:, :, None] == doc_here[:, None, :])
    intra_vals = jnp.exp(-rates[None, :, None, None] * distance[None, None])
    intra = jnp.where(linked[:, None], intra_vals, jnp.zeros_like(intra_vals))
    ahead = (offsets + 1).astype(float_kind)
    behind = (count - 1 - offsets).astype(float_kind)
    entry_vals = jnp.exp(-rates[None, None, :] * ahead[None, :, None])
    entry = jnp.where(
        (doc_here == doc_before[:, None])[:, :, None], entry_vals, jnp.zeros_like(entry_vals)
    )
    leaving_vals = jnp.exp(-rates[None, None, :] * behind[None, :, None])
    leaving = jnp.where(
        (doc_here == doc_last[:, None])[:, :, None], leaving_vals, jnp.zeros_like(leaving_vals)
    )
    length_value = jnp.asarray(count, dtype=float_kind)
    passing_vals = jnp.exp(-rates * length_value)[None, :] + jnp.zeros(
        (doc_last.shape[0], 1), float_kind
    )
    passing = jnp.where(
        (doc_last == doc_before)[:, None], passing_vals, jnp.zeros_like(passing_vals)
    )
    return (intra, entry, leaving, passing)


def block_out(per_head_queries, per_head_keys, per_head_values, tables, state_in):
    scores = (
        jnp.einsum("rthd,rshd->rhts", per_head_queries, per_head_keys, precision=FULL_PRECISION)
        * tables[0]
    )
    local_part = jnp.einsum("rhts,rshe->rthe", scores, per_head_values, precision=FULL_PRECISION)
    carried = (
        jnp.einsum("rthd,rhde->rthe", per_head_queries, state_in, precision=FULL_PRECISION)
        * tables[1][..., None]
    )
    return local_part + carried


def block_state(per_head_keys, per_head_values, tables):
    return jnp.einsum(
        "rshd,rshe->rhde",
        per_head_keys * tables[2][..., None],
        per_head_values,
        precision=FULL_PRECISION,
    )


def block_back(
    per_head_queries, per_head_keys, per_head_values, upstream, tables, state_in, state_grad
):
    intra, entry, leaving, passing = tables
    scores = (
        jnp.einsum("rthd,rshd->rhts", per_head_queries, per_head_keys, precision=FULL_PRECISION)
        * intra
    )
    score_grad = (
        jnp.einsum("rthe,rshe->rhts", upstream, per_head_values, precision=FULL_PRECISION) * intra
    )
    query_grad = jnp.einsum("rhts,rshd->rthd", score_grad, per_head_keys, precision=FULL_PRECISION)
    query_grad = (
        query_grad
        + jnp.einsum("rthe,rhde->rthd", upstream, state_in, precision=FULL_PRECISION)
        * entry[..., None]
    )
    key_grad = jnp.einsum("rhts,rthd->rshd", score_grad, per_head_queries, precision=FULL_PRECISION)
    key_grad = (
        key_grad
        + jnp.einsum("rshe,rhde->rshd", per_head_values, state_grad, precision=FULL_PRECISION)
        * leaving[..., None]
    )
    value_grad = jnp.einsum("rhts,rthe->rshe", scores, upstream, precision=FULL_PRECISION)
    value_grad = (
        value_grad
        + jnp.einsum("rshd,rhde->rshe", per_head_keys, state_grad, precision=FULL_PRECISION)
        * leaving[..., None]
    )
    return (query_grad, key_grad, value_grad)


def carry_forward(passing, local_state):

    def step_forward(turn_index, incoming):
        outgoing = passing[..., None, None] * incoming + local_state
        return passed_along(outgoing.astype(jnp.bfloat16), "seq", 1).astype(outgoing.dtype)

    return lax.fori_loop(0, lax.axis_size("seq") - 1, step_forward, jnp.zeros_like(local_state))


def carry_backward(passing, local_grad):

    def retreat(turn_index, incoming):
        outgoing = passing[..., None, None] * incoming + local_grad
        return passed_along(outgoing.astype(jnp.bfloat16), "seq", -1).astype(outgoing.dtype)

    return lax.fori_loop(0, lax.axis_size("seq") - 1, retreat, jnp.zeros_like(local_grad))


def reduce_grads(terms):
    pieces = (
        lax.psum_scatter(
            terms[0].astype(jnp.bfloat16), "dp", scatter_dimension=1, tiled=True
        ).astype(jnp.float32),
        lax.psum_scatter(
            terms[1].astype(jnp.bfloat16), "dp", scatter_dimension=0, tiled=True
        ).astype(jnp.float32),
        lax.psum_scatter(
            terms[2].astype(jnp.bfloat16), "dp", scatter_dimension=1, tiled=True
        ).astype(jnp.float32),
        lax.psum_scatter(
            terms[3].astype(jnp.bfloat16), "dp", scatter_dimension=0, tiled=True
        ).astype(jnp.float32),
    )
    return (
        lax.psum(pieces[0].astype(jnp.bfloat16), "seq").astype(jnp.float32),
        lax.psum(pieces[1].astype(jnp.bfloat16), "seq").astype(jnp.float32),
        lax.psum(pieces[2].astype(jnp.bfloat16), "seq").astype(jnp.float32),
        lax.psum(pieces[3].astype(jnp.bfloat16), "seq").astype(jnp.float32),
    )


def local(
    hidden_in,
    mixer_weights,
    channel_in_weights,
    channel_out_weights,
    decay_rates,
    doc_lengths,
    out_cotangent,
):
    rows, tokens, features = hidden_in.shape
    layers = mixer_weights.shape[0]
    heads = decay_rates.shape[1]
    head_dim = features // heads
    count = rows * tokens
    head_shape = (rows, tokens, heads, head_dim)
    start = lax.axis_index("seq") * jnp.asarray(tokens, dtype=jnp.int32)
    doc_ends = jnp.cumsum(doc_lengths, axis=1, dtype=jnp.int32)
    resid = hidden_in.astype(jnp.float32).reshape(count, features)
    layer_index = 0
    gathered = (
        mixer_weights[layer_index].astype(jnp.bfloat16),
        channel_in_weights[layer_index].astype(jnp.bfloat16),
        channel_out_weights[layer_index].astype(jnp.bfloat16),
    )
    mixer_full = lax.all_gather(gathered[0], "dp", axis=1, tiled=True)
    channel_full = lax.all_gather(gathered[1], "dp", axis=1, tiled=True)
    down_full = lax.all_gather(gathered[2], "dp", axis=0, tiled=True)
    normed, factor_in = rms_norm(resid)
    normed_low = normed.astype(jnp.bfloat16)
    projected = jnp.einsum(
        "nd,kde->kne", normed_low, mixer_full[:4], preferred_element_type=jnp.float32
    )
    query_pre = projected[0]
    key_pre = projected[1]
    value_pre = projected[2]
    gate_pre = projected[3]
    per_head_queries = (query_pre * jax.nn.sigmoid(query_pre)).reshape(head_shape)
    per_head_keys = (key_pre * jax.nn.sigmoid(key_pre)).reshape(head_shape)
    per_head_values = value_pre.reshape(head_shape)
    tables = decay_tables(decay_rates[layer_index], doc_ends, start, tokens)
    local_state = block_state(per_head_keys, per_head_values, tables)
    state_in = carry_forward(tables[3], local_state)
    mixed = block_out(per_head_queries, per_head_keys, per_head_values, tables, state_in).reshape(
        count, features
    )
    mixed_norm, factor_mix = rms_norm(mixed)
    gated = (mixed_norm * gate_pre).astype(jnp.bfloat16)
    after_mixer = resid + product(gated, mixer_full[4])
    normed_two, factor_two = rms_norm(after_mixer)
    normed_two_low = normed_two.astype(jnp.bfloat16)
    pair = jnp.einsum(
        "nd,kdf->knf", normed_two_low, channel_full, preferred_element_type=jnp.float32
    )
    glu = (pair[0] * pair[1]).astype(jnp.bfloat16)
    saved = [
        (
            mixer_full,
            channel_full,
            down_full,
            resid,
            factor_in,
            normed_low,
            query_pre,
            key_pre,
            gate_pre,
            per_head_queries,
            per_head_keys,
            per_head_values,
            tables,
            state_in,
            mixed,
            mixed_norm,
            factor_mix,
            gated,
            after_mixer,
            factor_two,
            normed_two_low,
            pair,
            glu,
        )
    ]
    resid = after_mixer + product(glu, down_full)
    block_output = resid.astype(jnp.bfloat16).reshape(rows, tokens, features)
    upstream = out_cotangent.astype(jnp.float32).reshape(count, features)
    mixer_list = []
    channel_list = []
    down_list = []
    for layer_index in reversed(range(layers)):
        (
            mixer_full,
            channel_full,
            down_full,
            resid_in,
            factor_in,
            normed_low,
            query_pre,
            key_pre,
            gate_pre,
            per_head_queries,
            per_head_keys,
            per_head_values,
            tables,
            state_in,
            mixed,
            mixed_norm,
            factor_mix,
            gated,
            after_mixer,
            factor_two,
            normed_two_low,
            pair,
            glu,
        ) = saved[layer_index]
        branch_low = upstream.astype(jnp.bfloat16)
        down_term = jnp.einsum("nf,nd->fd", glu, branch_low, preferred_element_type=jnp.float32)
        glu_grad = (
            jnp.einsum("nd,fd->nf", branch_low, down_full, preferred_element_type=jnp.float32)
            .astype(jnp.bfloat16)
            .astype(jnp.float32)
        )
        pair_grad = jnp.stack([glu_grad * pair[1], glu_grad * pair[0]]).astype(jnp.bfloat16)
        channel_term = jnp.einsum(
            "nd,knf->kdf", normed_two_low, pair_grad, preferred_element_type=jnp.float32
        )
        two_grad = jnp.einsum(
            "knf,kdf->nd", pair_grad, channel_full, preferred_element_type=jnp.float32
        )
        upstream_mid = upstream + norm_back(after_mixer, factor_two, two_grad)
        mixer_low = upstream_mid.astype(jnp.bfloat16)
        out_term = jnp.einsum("nd,ne->de", gated, mixer_low, preferred_element_type=jnp.float32)
        gated_grad = (
            jnp.einsum("ne,de->nd", mixer_low, mixer_full[4], preferred_element_type=jnp.float32)
            .astype(jnp.bfloat16)
            .astype(jnp.float32)
        )
        gate_grad = gated_grad * mixed_norm
        mixed_grad = norm_back(mixed, factor_mix, gated_grad * gate_pre).reshape(head_shape)
        local_grad = jnp.einsum(
            "rthd,rthe->rhde",
            per_head_queries * tables[1][..., None],
            mixed_grad,
            precision=FULL_PRECISION,
        )
        state_grad = carry_backward(tables[3], local_grad)
        query_grad, key_grad, value_grad = block_back(
            per_head_queries,
            per_head_keys,
            per_head_values,
            mixed_grad,
            tables,
            state_in,
            state_grad,
        )
        proj_grad = jnp.stack(
            [
                query_grad.reshape(count, features) * swish_slope(query_pre),
                key_grad.reshape(count, features) * swish_slope(key_pre),
                value_grad.reshape(count, features),
                gate_grad,
            ]
        ).astype(jnp.bfloat16)
        four_term = jnp.einsum(
            "nd,kne->kde", normed_low, proj_grad, preferred_element_type=jnp.float32
        )
        one_grad = jnp.einsum(
            "kne,kde->nd", proj_grad, mixer_full[:4], preferred_element_type=jnp.float32
        )
        upstream = upstream_mid + norm_back(resid_in, factor_in, one_grad)
        summed = reduce_grads((four_term, out_term, channel_term, down_term))
        mixer_list.append(jnp.concatenate([summed[0], summed[1][None]], axis=0))
        channel_list.append(summed[2])
        down_list.append(summed[3])
    mixer_gradient = jnp.stack(mixer_list[::-1])
    channel_in_gradient = jnp.stack(channel_list[::-1])
    channel_out_gradient = jnp.stack(down_list[::-1])
    input_gradient = upstream.reshape(rows, tokens, features)
    return (block_output, input_gradient, mixer_gradient, channel_in_gradient, channel_out_gradient)


def solution(mesh):
    in_specs = (
        P("dp", "seq", None),
        P(None, None, "dp", None),
        P(None, None, "dp", None),
        P(None, "dp", None),
        P(),
        P("dp", None),
        P("dp", "seq", None),
    )
    out_specs = (
        P("dp", "seq", None),
        P("dp", "seq", None),
        P(None, None, "dp", None),
        P(None, None, "dp", None),
        P(None, "dp", None),
    )
    return jax.shard_map(local, mesh=mesh, in_specs=in_specs, out_specs=out_specs, check_vma=False)
```

profile of v0, /device:TPU:0, one launch (start us, length us, event | category | flops | bytes accessed | tf_op | source)
XLA Modules:
  0.0 966.9 jit_solution(12912789637610193381)
XLA Ops:
  26.6 51.9 %all-gather.7.cloned.1.call-done = bf16[1,5,1024,1024]{2,3,1,0:T(8,128)(2,1)} async-done(((bf16[1,5,128,1024]{2,3,1,0:T(8,128)(2,1)}), bf16[1,5,1024,1024]{2,3,1,0:T(8,128)(2,1)}) %all-gather.7.cloned.1.call-update) | async-done | bytes 10485776 | tf_op jit(solution)/shard_map/all_gather | solution.py:193
  78.5 16.3 %convolution_bitcast_fusion = f32[4,1024,1024]{1,2,0:T(8,128)} fusion(bf16[1,5,1024,1024]{2,3,1,0:T(8,128)(2,1)} %all-gather.7.cloned.1.call-done, bf16[1024,1024]{1,0:T(8,128)(2,1)} %fusion.65), kind=kOutput, calls=%fused_computation.30 | convolution fusion | flops 8589934592 | bytes 27262976 | tf_op jit(solution)/shard_map/nd,kde->kne/dot_general | solution.py:198
  94.7 10.2 %fusion.120 = (f32[1,1024,1024]{1,2,0:T(8,128)}, f32[1,1024,1024]{1,2,0:T(8,128)}, f32[1,1024,1024]{1,2,0:T(8,128)}) fusion(f32[4,1024,1024]{1,2,0:T(8,128)} %convolution_bitcast_fusion), kind=kLoop, calls=%fused_computation.166 | loop fusion | bytes 25165824 | tf_op jit(solution)/shard_map/slice | solution.py:201
  111.5 7.4 copy.119
  125.5 6.8 squeeze.12
  132.2 8.6 fusion.69
  140.8 48.7 %while.22 = (s32[]{:T(128)}, f32[2,8,128,128]{3,2,1,0:T(8,128)S(1)}, f32[2,8,128,128]{3,2,1,0:T(8,128)S(1)}, f32[8]{0:T(128)S(1)}, pred[2]{0:T(512)(128)(4,1)S(1)}, /*index=5*/s32[]{:T(128)}, s32[]{:T(128)}) while((s32[]{:T(128)}, f32[2,8,128,128]{3,2,1,0:T(8,128)S(1)}, f32[2,8,128,128]{3,2,1,0:T(8,128)S(1)}, f32[8]{0:T(128)S(1)}, ...), condition=%wide.region_5.6_spmd.clone, body=%wide.region_4.5_spmd.clone.sunk | while | flops 1310739 | bytes 6291745 | solution.py:134
  145.3 11.9 %collective-permute-done = bf16[2,8,128,128]{3,2,1,0:T(8,128)(2,1)S(1)} collective-permute-done((bf16[2,8,128,128]{3,2,1,0:T(8,128)(2,1)}, bf16[2,8,128,128]{3,2,1,0:T(8,128)(2,1)S(1)}, u32[]{:S(2)}, u32[]{:S(2)}) %collective-permute-start) | collective-permute-done | bytes 524320 | tf_op jit(solution)/shard_map/while/body/eval_jaxpr/ppermute | solution.py:13
  162.7 11.1 %collective-permute-done = bf16[2,8,128,128]{3,2,1,0:T(8,128)(2,1)S(1)} collective-permute-done((bf16[2,8,128,128]{3,2,1,0:T(8,128)(2,1)}, bf16[2,8,128,128]{3,2,1,0:T(8,128)(2,1)S(1)}, u32[]{:S(2)}, u32[]{:S(2)}) %collective-permute-start) | collective-permute-done | bytes 524320 | tf_op jit(solution)/shard_map/while/body/eval_jaxpr/ppermute | solution.py:13
  179.2 10.1 %collective-permute-done = bf16[2,8,128,128]{3,2,1,0:T(8,128)(2,1)S(1)} collective-permute-done((bf16[2,8,128,128]{3,2,1,0:T(8,128)(2,1)}, bf16[2,8,128,128]{3,2,1,0:T(8,128)(2,1)S(1)}, u32[]{:S(2)}, u32[]{:S(2)}) %collective-permute-start) | collective-permute-done | bytes 524320 | tf_op jit(solution)/shard_map/while/body/eval_jaxpr/ppermute | solution.py:13
  189.6 9.2 fusion.119
  198.8 17.2 %fusion.118 = f32[2,8,512,512]{3,2,1,0:T(8,128)} fusion(f32[2,512,8,128]{1,0,3,2:T(2,128)S(1)} %copy-done.14, f32[2,512,8,128]{1,0,3,2:T(2,128)S(1)} %copy-done.13), kind=kOutput, calls=%fused_computation.164 | convolution fusion | flops 6450839552 | bytes 25165824 | tf_op jit(solution)/shard_map/rthd,rshd->rhts/dot_general | solution.py:76
  216.0 23.7 %multiply_reduce_fusion.2 = (f32[2,512]{1,0:T(2,128)S(1)}, f32[2,512,8,128]{1,3,2,0:T(8,128)}) fusion(f32[2,512,8]{1,2,0:T(8,128)S(1)} %get-tuple-element.166, f32[2,8,128,512]{3,2,1,0:T(8,128)} %fusion.119, f32[2,512,8,128]{3,1,2,0:T(8,128)} %copy.119, f32[2,8,512,512]{3,2,1,0:T(8,128)} %fusion.118, f32[8,512,512]{2,1,0:T(8,128)} %multiply_exponential_fusion, ...), kind=kOutput, calls=%fused_computation.99 | convolution fusion | flops 6455032832 | bytes 38309888 | tf_op jit(solution)/shard_map/rhts,rshe->rthe/dot_general | solution.py:79
  239.7 7.5 copy.123
  247.3 6.6 reshape.339
  259.4 7.6 multiply_reduce_fusion.1
  267.0 20.9 %fusion.19 = f32[2,1024,2816]{2,1,0:T(8,128)} fusion(bf16[1,2,1024,2816]{3,2,1,0:T(8,128)(2,1)} %all-gather.9.cloned.1.call-done, f32[1024,1024]{1,0:T(8,128)} %get-tuple-element.159, f32[1024]{0:T(1024)S(1)} %get-tuple-element.149), kind=kOutput, calls=%fused_computation.29 | convolution fusion | flops 11813257216 | bytes 38801408 | tf_op jit(solution)/shard_map/nd,kdf->knf/dot_general | solution.py:219
  287.9 14.9 %fusion.41 = (bf16[1,1024,2816]{2,1,0:T(8,128)(2,1)}, bf16[1,1024,2816]{2,1,0:T(8,128)(2,1)}) fusion(f32[2,1024,2816]{2,1,0:T(8,128)} %fusion.19, bf16[1024,1024]{1,0:T(8,128)(2,1)S(1)} %bitcast.231, bf16[1,2816,1024]{2,1,0:T(8,128)(2,1)} %all-gather.11.cloned.1.call-done), kind=kOutput, calls=%fused_computation.52 | convolution fusion | flops 5922881536 | bytes 42467328 | tf_op jit(solution)/shard_map/nd,fd->nf/dot_general | solution.py:285
  302.9 20.3 %fusion.62 = (f32[1024]{0:T(1024)S(1)}, f32[1024,1024,1]{1,0,2:T(8,128)}) fusion(f32[1024,1024]{1,0:T(8,128)} %get-tuple-element.159, bf16[1,2,1024,2816]{3,2,1,0:T(8,128)(2,1)} %all-gather.9.cloned.1.call-done, bf16[1,1024,2816]{2,1,0:T(8,128)(2,1)} %get-tuple-element.140, bf16[1,1024,2816]{2,1,0:T(8,128)(2,1)} %get-tuple-element.139), kind=kOutput, calls=%fused_computation.79 | convolution fusion | flops 11819023360 | bytes 31461376 | tf_op jit(solution)/shard_map/knf,kdf->nd/dot_general | solution.py:293
  327.9 7.2 multiply_reduce_fusion
  341.4 6.6 reshape.344
  348.0 19.9 %fusion.8 = f32[2,8,128,512]{3,2,1,0:T(8,128)} fusion(f32[2,8,512,512]{3,2,1,0:T(8,128)} %fusion.118, f32[8,512,512]{2,1,0:T(8,128)} %multiply_exponential_fusion, pred[2,512,512]{2,1,0:T(8,128)(4,1)S(1)} %compare_and_fusion, f32[2,512,8,128]{1,0,3,2:T(2,128)} %reshape.344), kind=kOutput, calls=%fused_computation.12 | convolution fusion | flops 6450839552 | bytes 34078720 | tf_op jit(solution)/shard_map/rhts,rthe->rshe/dot_general | solution.py:119
  367.9 8.9 fusion.67
  376.8 16.0 %fusion.74 = f32[2,8,512,512]{3,2,1,0:T(8,128)} fusion(f32[2,512,8,128]{3,1,2,0:T(8,128)S(1)} %copy-done.5, f32[2,512,8,128]{1,0,3,2:T(2,128)S(1)} %copy-done.6), kind=kOutput, calls=%fused_computation.107 | convolution fusion | flops 6442450944 | bytes 25165824 | tf_op jit(solution)/shard_map/rthe,rshe->rhts/dot_general | solution.py:105
  398.8 43.1 %while.23 = (s32[]{:T(128)}, f32[2,8,128,128]{3,2,1,0:T(8,128)S(1)}, f32[2,8,128,128]{3,2,1,0:T(8,128)S(1)}, f32[8]{0:T(128)S(1)}, pred[2]{0:T(512)(128)(4,1)S(1)}, /*index=5*/s32[]{:T(128)}, s32[]{:T(128)}) while((s32[]{:T(128)}, f32[2,8,128,128]{3,2,1,0:T(8,128)S(1)}, f32[2,8,128,128]{3,2,1,0:T(8,128)S(1)}, f32[8]{0:T(128)S(1)}, ...), condition=%wide.region_11.12_spmd.clone, body=%wide.region_10.11_spmd.clone.sunk | while | flops 1310739 | bytes 6291745 | solution.py:143
  401.1 13.0 %collective-permute-done.1 = bf16[2,8,128,128]{3,2,1,0:T(8,128)(2,1)S(1)} collective-permute-done((bf16[2,8,128,128]{3,2,1,0:T(8,128)(2,1)}, bf16[2,8,128,128]{3,2,1,0:T(8,128)(2,1)S(1)}, u32[]{:S(2)}, u32[]{:S(2)}) %collective-permute-start.1) | collective-permute-done | bytes 524320 | tf_op jit(solution)/shard_map/while/body/eval_jaxpr/ppermute | solution.py:13
  416.6 11.7 %collective-permute-done.1 = bf16[2,8,128,128]{3,2,1,0:T(8,128)(2,1)S(1)} collective-permute-done((bf16[2,8,128,128]{3,2,1,0:T(8,128)(2,1)}, bf16[2,8,128,128]{3,2,1,0:T(8,128)(2,1)S(1)}, u32[]{:S(2)}, u32[]{:S(2)}) %collective-permute-start.1) | collective-permute-done | bytes 524320 | tf_op jit(solution)/shard_map/while/body/eval_jaxpr/ppermute | solution.py:13
  430.7 10.8 %collective-permute-done.1 = bf16[2,8,128,128]{3,2,1,0:T(8,128)(2,1)S(1)} collective-permute-done((bf16[2,8,128,128]{3,2,1,0:T(8,128)(2,1)}, bf16[2,8,128,128]{3,2,1,0:T(8,128)(2,1)S(1)}, u32[]{:S(2)}, u32[]{:S(2)}) %collective-permute-start.1) | collective-permute-done | bytes 524320 | tf_op jit(solution)/shard_map/while/body/eval_jaxpr/ppermute | solution.py:13
  441.9 8.1 fusion.123
  459.8 28.1 %fusion.11 = f32[2,8,128,512]{3,2,1,0:T(8,128)} fusion(f32[2,8,512,512]{3,2,1,0:T(8,128)} %fusion.74, f32[8,512,512]{2,1,0:T(8,128)} %multiply_exponential_fusion, pred[2,512,512]{2,1,0:T(8,128)(4,1)S(1)} %compare_and_fusion, f32[2,512,8,128]{1,0,3,2:T(2,128)} %squeeze.13), kind=kOutput, calls=%fused_computation.15 | convolution fusion | flops 6455033856 | bytes 34078720 | tf_op jit(solution)/shard_map/rhts,rshd->rthd/dot_general | solution.py:107
  487.8 8.5 fusion.58
  501.6 6.6 reshape.345
  508.2 21.7 %fusion.57 = f32[2,512,8,128]{1,3,2,0:T(8,128)} fusion(f32[2,8,128,512]{3,2,1,0:T(8,128)} %fusion.123, f32[2,8,512,512]{3,2,1,0:T(8,128)} %fusion.74, f32[8,512,512]{2,1,0:T(8,128)} %multiply_exponential_fusion, pred[2,512,512]{2,1,0:T(8,128)(4,1)S(1)} %compare_and_fusion, f32[2,512,8]{1,2,0:T(8,128)S(1)} %copy-done.28, f32[2,512,8,128]{1,0,3,2:T(2,128)} %squeeze.12), kind=kOutput, calls=%fused_computation.70 | convolution fusion | flops 6457131008 | bytes 38305792 | tf_op jit(solution)/shard_map/rhts,rthd->rshd/dot_general | solution.py:113
  529.9 7.5 copy.131
  537.4 6.6 reshape.346
  544.1 8.3 multiply_convert_fusion.2
  554.5 11.0 %convert_bitcast_fusion.1 = bf16[4,1024,1024]{1,2,0:T(8,128)(2,1)} fusion(bf16[1024,1024]{1,0:T(8,128)(2,1)S(1)} %copy-done.22, bf16[1,1024,1024]{1,2,0:T(8,128)(2,1)S(1)} %copy-done.19, bf16[1,1024,1024]{1,2,0:T(8,128)(2,1)S(1)} %copy-done.23, bf16[1,1024,1024]{1,2,0:T(8,128)(2,1)S(1)} %get-tuple-element.142, bf16[1,1024,1024]{1,2,0:T(8,128)(2,1)S(1)} %get-tuple-element.141), kind=kOutput, calls=%fused_computation.33 | convolution fusion | flops 8606711808 | bytes 18874368 | tf_op jit(solution)/shard_map/nd,kne->kde/dot_general | solution.py:330
  565.5 15.0 %copy.151 = bf16[4,1024,1024]{2,0,1:T(4,128)(2,1)} copy(bf16[4,1024,1024]{1,2,0:T(8,128)(2,1)} %convert_bitcast_fusion.1) | data formatting | bytes 16777216
  580.5 12.3 %copy.160 = bf16[128,8,4,1024]{3,1,2,0:T(8,128)(2,1)} copy(bf16[128,8,4,1024]{3,2,1,0:T(4,128)(2,1)} %bitcast.226) | data formatting | bytes 16777216
  592.8 19.1 %convert_bitcast_fusion = bf16[2,1024,2816]{1,2,0:T(8,128)(2,1)} fusion(bf16[1,1024,2816]{2,1,0:T(8,128)(2,1)} %get-tuple-element.140, bf16[1,1024,2816]{2,1,0:T(8,128)(2,1)} %get-tuple-element.139, f32[1024,1024]{1,0:T(8,128)} %get-tuple-element.159, f32[1024]{0:T(1024)S(1)} %get-tuple-element.149), kind=kOutput, calls=%fused_computation.28 | convolution fusion | flops 11824791552 | bytes 27267072 | tf_op jit(solution)/shard_map/nd,knf->kdf/dot_general | solution.py:290
  611.9 29.1 %copy.155 = bf16[2,1024,2816]{2,0,1:T(2,128)(2,1)} copy(bf16[2,1024,2816]{1,2,0:T(8,128)(2,1)} %convert_bitcast_fusion) | data formatting | bytes 23068672
  641.0 11.4 %copy.161 = bf16[128,8,2,2816]{3,1,2,0:T(8,128)(2,1)} copy(bf16[128,8,2,2816]{3,2,1,0:T(2,128)(2,1)} %bitcast.223) | data formatting | bytes 23068672
  654.0 15.9 %fusion.45 = bf16[2816,1024]{1,0:T(8,128)(2,1)} fusion(bf16[1024,1024]{1,0:T(8,128)(2,1)S(1)} %bitcast.232, f32[2,1024,2816]{2,1,0:T(8,128)} %fusion.19), kind=kOutput, calls=%fused_computation.56 | convolution fusion | flops 5914230784 | bytes 30932992 | tf_op jit(solution)/shard_map/nf,nd->fd/dot_general | solution.py:283
  676.2 76.9 %reduce-scatter.17.cloned.1.call-done = bf16[128,5632]{1,0:T(8,128)(2,1)} async-done(((bf16[1024,5632]{1,0:T(8,128)(2,1)}), bf16[128,5632]{1,0:T(8,128)(2,1)}) %reduce-scatter.17.cloned.1.call-update) | async-done | bytes 1441808
  759.6 56.0 %reduce-scatter.11.cloned.1.call-done = bf16[352,1024]{1,0:T(8,128)(2,1)} async-done(((bf16[2816,1024]{1,0:T(8,128)(2,1)}), bf16[352,1024]{1,0:T(8,128)(2,1)}) %reduce-scatter.11.cloned.1.call-update) | async-done | bytes 720912 | tf_op jit(solution)/shard_map/reduce_scatter | solution.py:157
  815.7 15.1 %fusion.54 = (f32[1024]{0:T(1024)S(1)}, f32[1024,1024,1]{1,0,2:T(8,128)S(1)}) fusion(bf16[2,512,1024]{2,1,0:T(8,128)(2,1)S(1)} %copy-done.12, bf16[1,5,1024,1024]{2,3,1,0:T(8,128)(2,1)} %all-gather.7.cloned.1.call-done, bf16[1,1024,1024]{1,2,0:T(8,128)(2,1)} %get-tuple-element.147, bf16[1,1024,1024]{1,2,0:T(8,128)(2,1)} %stack_reshape.4, ...), kind=kOutput, calls=%fused_computation.65 | convolution fusion | flops 8605662208 | bytes 23072768 | tf_op jit(solution)/shard_map/kne,kde->nd/dot_general | solution.py:333
  834.4 13.7 %add_convert_fusion = bf16[1024,1024]{1,0:T(8,128)(2,1)} fusion(f32[1024,1024]{1,0:T(8,128)S(1)} %copy-done.17, bf16[1,2816,1024]{2,1,0:T(8,128)(2,1)} %all-gather.11.cloned.1.call-done, f32[2,1024,2816]{2,1,0:T(8,128)} %fusion.19), kind=kOutput, calls=%fused_computation.95 | convolution fusion | flops 5913444352 | bytes 35127296 | tf_op jit(solution)/shard_map/dot_general | solution.py:17
  848.1 103.7 %all-reduce.3.cloned.1.call-done = (bf16[1,2,128,2816]{2,3,1,0:T(8,128)(2,1)}, bf16[1,128,1024]{1,2,0:T(8,128)(2,1)}, bf16[4,128,1024]{1,2,0:T(8,128)(2,1)}, bf16[1,352,1024]{2,1,0:T(8,128)(2,1)}) async-done(((bf16[1,2,128,2816]{2,3,1,0:T(8,128)(2,1)}, bf16[1,128,1024]{1,2,0:T(8,128)(2,1)}, bf16[4,128,1024]{1,2,0:T(8,128)(2,1)}, bf16[1,352,1024]{2,1,0:T(8,128)(2,1)}), (bf16[1,2,128,2816]{2,3,1,0:T(8,128)(2,1)}, ...) | async-done | bytes 3473424 | tf_op jit(solution)/shard_map/psum | solution.py:164
  (169 shorter events, 120.6 us)
Async XLA Ops:
  7.2 71.3 %all-gather.7.cloned.1.call-start = ((), (), s32[]{:S(2)}) async-start(), calls=%async_computation.5 | async-start | bytes 11796480 | tf_op jit(solution)/shard_map/all_gather | solution.py:193
  10.0 7.0 copy-start.10
  10.0 256.9 %all-gather.9.cloned.1.call-start = ((), (), s32[]{:S(2)}) async-start(), calls=%async_computation.6 | async-start | bytes 12976128 | tf_op jit(solution)/shard_map/all_gather | solution.py:194
  13.3 274.6 %all-gather.11.cloned.1.call-start = ((), (), s32[]{:S(2)}) async-start(), calls=%async_computation.7 | async-start | bytes 6488064 | tf_op jit(solution)/shard_map/all_gather | solution.py:195
  15.7 3.6 copy-start.36
  15.7 3.6 copy-start.35
  15.7 654.9 %reduce-scatter.15.cloned.1.call-start = ((), (), s32[]{:S(2)}) async-start(), calls=%async_computation.9 | async-start | bytes 2359296
  17.5 1.7 copy-start.29
  26.6 105.7 %copy-start.27 = (f32[2,512,8]{1,2,0:T(8,128)}, f32[2,512,8]{1,2,0:T(8,128)S(1)}, u32[]{:S(2)}) copy-start(f32[2,512,8]{1,2,0:T(8,128)S(1)} %get-tuple-element.167) | copy-start | bytes 98308
  141.9 15.3 %collective-permute-start = (bf16[2,8,128,128]{3,2,1,0:T(8,128)(2,1)}, bf16[2,8,128,128]{3,2,1,0:T(8,128)(2,1)S(1)}, u32[]{:S(2)}, u32[]{:S(2)}) collective-permute-start(bf16[2,8,128,128]{3,2,1,0:T(8,128)(2,1)} %fusion.136), channel_id=1, source_target_pairs={{0,8},{8,16},{16,24},{1,9},{9,17},{17,25},{2,10},{10,18},{18,26},{... | collective-permute-start | bytes 1572872 | tf_op jit(solution)/shard_map/while/body/eval_jaxpr/ppermute | solution.py:13
  158.4 15.4 %collective-permute-start = (bf16[2,8,128,128]{3,2,1,0:T(8,128)(2,1)}, bf16[2,8,128,128]{3,2,1,0:T(8,128)(2,1)S(1)}, u32[]{:S(2)}, u32[]{:S(2)}) collective-permute-start(bf16[2,8,128,128]{3,2,1,0:T(8,128)(2,1)} %fusion.136), channel_id=1, source_target_pairs={{0,8},{8,16},{16,24},{1,9},{9,17},{17,25},{2,10},{10,18},{18,26},{... | collective-permute-start | bytes 1572872 | tf_op jit(solution)/shard_map/while/body/eval_jaxpr/ppermute | solution.py:13
  174.9 14.5 %collective-permute-start = (bf16[2,8,128,128]{3,2,1,0:T(8,128)(2,1)}, bf16[2,8,128,128]{3,2,1,0:T(8,128)(2,1)S(1)}, u32[]{:S(2)}, u32[]{:S(2)}) collective-permute-start(bf16[2,8,128,128]{3,2,1,0:T(8,128)(2,1)} %fusion.136), channel_id=1, source_target_pairs={{0,8},{8,16},{16,24},{1,9},{9,17},{17,25},{2,10},{10,18},{18,26},{... | collective-permute-start | bytes 1572872 | tf_op jit(solution)/shard_map/while/body/eval_jaxpr/ppermute | solution.py:13
  189.5 9.2 copy-start.8
  189.5 9.2 copy-start.31
  189.5 9.2 copy-start.33
  189.5 9.2 copy-start.13
  189.5 9.2 copy-start.14
  253.9 5.5 copy-start.11
  253.9 5.5 copy-start.16
  267.0 20.9 %copy-start.24 = (bf16[2,512,1024]{2,1,0:T(8,128)(2,1)S(1)}, bf16[2,512,1024]{2,1,0:T(8,128)(2,1)}, u32[]{:S(2)}) copy-start(bf16[2,512,1024]{2,1,0:T(8,128)(2,1)} %param.17) | copy-start | bytes 6291460
  323.1 4.7 copy-start
  327.8 7.2 copy-start.2
  367.9 8.9 copy-start.5
  367.9 8.9 copy-start.6
  376.8 16.0 %copy-start.1 = (f32[128,8,2,512]{3,1,2,0:T(8,128)S(1)}, f32[128,8,2,512]{3,1,2,0:T(8,128)}, u32[]{:S(2)}) copy-start(f32[128,8,2,512]{3,1,2,0:T(8,128)} %copy.159) | copy-start | bytes 12582916
  376.8 16.0 %copy-start.3 = (f32[1024,1024]{1,0:T(8,128)S(1)}, f32[1024,1024]{1,0:T(8,128)}, u32[]{:S(2)}) copy-start(f32[1024,1024]{1,0:T(8,128)} %copy-done.2) | copy-start | bytes 12582916
  392.8 5.9 copy-start.7
  392.8 5.9 copy-start.32
  392.8 5.9 copy-start.34
  399.8 14.3 %collective-permute-start.1 = (bf16[2,8,128,128]{3,2,1,0:T(8,128)(2,1)}, bf16[2,8,128,128]{3,2,1,0:T(8,128)(2,1)S(1)}, u32[]{:S(2)}, u32[]{:S(2)}) collective-permute-start(bf16[2,8,128,128]{3,2,1,0:T(8,128)(2,1)} %fusion.137), channel_id=1, source_target_pairs={{8,0},{16,8},{24,16},{9,1},{17,9},{25,17},{10,2},{18,10},{26,18},{... | collective-permute-start | bytes 1572872 | tf_op jit(solution)/shard_map/while/body/eval_jaxpr/ppermute | solution.py:13
  415.3 13.0 %collective-permute-start.1 = (bf16[2,8,128,128]{3,2,1,0:T(8,128)(2,1)}, bf16[2,8,128,128]{3,2,1,0:T(8,128)(2,1)S(1)}, u32[]{:S(2)}, u32[]{:S(2)}) collective-permute-start(bf16[2,8,128,128]{3,2,1,0:T(8,128)(2,1)} %fusion.137), channel_id=1, source_target_pairs={{8,0},{16,8},{24,16},{9,1},{17,9},{25,17},{10,2},{18,10},{26,18},{... | collective-permute-start | bytes 1572872 | tf_op jit(solution)/shard_map/while/body/eval_jaxpr/ppermute | solution.py:13
  429.5 12.1 %collective-permute-start.1 = (bf16[2,8,128,128]{3,2,1,0:T(8,128)(2,1)}, bf16[2,8,128,128]{3,2,1,0:T(8,128)(2,1)S(1)}, u32[]{:S(2)}, u32[]{:S(2)}) collective-permute-start(bf16[2,8,128,128]{3,2,1,0:T(8,128)(2,1)} %fusion.137), channel_id=1, source_target_pairs={{8,0},{16,8},{24,16},{9,1},{17,9},{25,17},{10,2},{18,10},{26,18},{... | collective-permute-start | bytes 1572872 | tf_op jit(solution)/shard_map/while/body/eval_jaxpr/ppermute | solution.py:13
  441.9 8.1 copy-start.15
  441.9 8.1 copy-start.18
  441.9 8.1 copy-start.28
  459.8 28.1 %copy-start.9 = (f32[2,8,128,128]{3,2,1,0:T(8,128)S(1)}, f32[2,8,128,128]{3,2,1,0:T(8,128)}, u32[]{:S(2)}) copy-start(f32[2,8,128,128]{3,2,1,0:T(8,128)} %copy-done.8) | copy-start | bytes 3145732
  544.0 10.4 %copy-start.19 = (bf16[1,1024,1024]{1,2,0:T(8,128)(2,1)S(1)}, bf16[1,1024,1024]{1,2,0:T(8,128)(2,1)}, u32[]{:S(2)}) copy-start(bf16[1,1024,1024]{1,2,0:T(8,128)(2,1)} %get-tuple-element.147) | copy-start | bytes 6291460
  544.0 128.4 %reduce-scatter.13.cloned.1.call-start = ((), (), s32[]{:S(2)}) async-start(), calls=%async_computation.8 | async-start | bytes 9437184
  544.1 10.4 %copy-start.22 = (bf16[1024,1024]{1,0:T(8,128)(2,1)S(1)}, bf16[1024,1024]{1,0:T(8,128)(2,1)}, u32[]{:S(2)}) copy-start(bf16[1024,1024]{1,0:T(8,128)(2,1)} %fusion.65) | copy-start | bytes 6291460
  544.1 10.4 %copy-start.23 = (bf16[1,1024,1024]{1,2,0:T(8,128)(2,1)S(1)}, bf16[1,1024,1024]{1,2,0:T(8,128)(2,1)}, u32[]{:S(2)}) copy-start(bf16[1,1024,1024]{1,2,0:T(8,128)(2,1)} %stack_reshape.4) | copy-start | bytes 6291460
  552.4 2.0 copy-start.21
  592.7 160.4 %reduce-scatter.17.cloned.1.call-start = ((), (), s32[]{:S(2)}) async-start(), calls=%async_computation.10 | async-start | bytes 12976128
  652.4 163.2 %reduce-scatter.11.cloned.1.call-start = ((), (), s32[]{:S(2)}) async-start(), calls=%async_computation.4 | async-start | bytes 6488064 | tf_op jit(solution)/shard_map/reduce_scatter | solution.py:157
  670.0 281.8 %all-reduce.3.cloned.1.call-start = ((), (), s32[]{:S(2)}) async-start(), calls=%async_computation.11 | async-start | bytes 6946816 | tf_op jit(solution)/shard_map/psum | solution.py:164
  676.2 139.5 %copy-start.12 = (bf16[2,512,1024]{2,1,0:T(8,128)(2,1)S(1)}, bf16[2,512,1024]{2,1,0:T(8,128)(2,1)}, u32[]{:S(2)}) copy-start(bf16[2,512,1024]{2,1,0:T(8,128)(2,1)} %param.11) | copy-start | bytes 6291460
  815.7 15.1 %copy-start.4 = (f32[1024,1024]{1,0:T(8,128)S(1)}, f32[1024,1024]{1,0:T(8,128)}, u32[]{:S(2)}) copy-start(f32[1024,1024]{1,0:T(8,128)} %copy-done.2) | copy-start | bytes 12582916
  830.9 3.5 copy-start.17
  953.3 5.1 copy-start.26
  (3 other events, 3.6 us)
Sparse Core Ops, SparseCore 0:
  10.4 67.9 all-gather.6
  80.9 67.6 all-gather.8
  150.5 43.3 all-gather.10
  544.1 40.0 reduce-scatter.14
  592.9 70.0 reduce-scatter.12
  666.3 86.8 reduce-scatter.16
  756.6 59.0 reduce-scatter.10
  819.1 132.6 all-reduce.2
where the time goes:
time: 978 us; the launch traced here: 967 us
  waiting for transfers between devices  357 us (37%)
  matrix products  343 us (35%)
  local copies, waits for them, and re-layouts  187 us (19%)
  other arithmetic  47.8 us (5%)
  starting transfers between devices  16.2 us (2%)
  between operations  15.2 us (2%)
    psum x1, waiting for transfers between devices, reduce_grads(): lax.psum(pieces[2].astype(jnp.bfloat16), 'seq').astype(jnp.float32)  104 us
    unnamed x89, local copies, waits for them, and re-layouts  98 us
    unnamed x11, waiting for transfers between devices  77.1 us
    ppermute x6, waiting for transfers between devices, passed_along(): lax.ppermute(value, axis, [(source, source + steps) for source in range(l...  68.6 us
    reduce_scatter x1, waiting for transfers between devices, reduce_grads(): lax.psum_scatter(terms[3].astype(jnp.bfloat16), 'dp', scatter_dimension=0...  56 us
    all_gather x1, waiting for transfers between devices, local(): mixer_full = lax.all_gather(gathered[0], 'dp', axis=1, tiled=True)  51.9 us
    dot_general x1, matrix products, block_back(): jnp.einsum('rhts,rshd->rthd', score_grad, per_head_keys, precision=FULL_P...  28.1 us
    dot_general x1, matrix products, block_out(): jnp.einsum('rhts,rshe->rthe', scores, per_head_values, precision=FULL_PRE...  23.7 us
  transfers between devices with their start and end apart: 14, of which 10 were waited for; matrix products, arithmetic and copies ran while one was open for 36% of the time, Pallas kernels for 0%

commit v1 on v0

--- a/solution.py
+++ b/solution.py
@@ -5,6 +5,20 @@
 
 EPS = 1e-06
 FULL_PRECISION = lax.Precision.HIGHEST
+
+
+def close_wall_over_axis(body):
+    t1, prior = (lax.axis_size("dp"), lax.axis_index("dp"))
+    ready, top = (body, 1)
+    while top < t1:
+        out_arr = lax.ppermute(
+            ready, axis_name="dp", perm=[(hop_no, hop_no ^ top) for hop_no in range(t1)]
+        )
+        a_next = jnp.concatenate([ready, out_arr], axis=1)
+        current_block = jnp.concatenate([out_arr, ready], axis=1)
+        ready = jnp.where(prior & top == 0, a_next, current_block)
+        top = 2 * top
+    return ready
 
 
 def passed_along(value, axis, steps):
@@ -190,7 +204,7 @@
         channel_in_weights[layer_index].astype(jnp.bfloat16),
         channel_out_weights[layer_index].astype(jnp.bfloat16),
     )
-    mixer_full = lax.all_gather(gathered[0], "dp", axis=1, tiled=True)
+    mixer_full = close_wall_over_axis(gathered[0])
     channel_full = lax.all_gather(gathered[1], "dp", axis=1, tiled=True)
     down_full = lax.all_gather(gathered[2], "dp", axis=0, tiled=True)
     normed, factor_in = rms_norm(resid)

time: 978 us -> 1170 us (1.20)
  waiting for transfers between devices: 357 us -> 529 us
  other arithmetic: 47.8 us -> 62.1 us
    ppermute x0 -> x3, waiting for transfers between devices: none -> 233 us  [close_wall_over_axis(): lax.ppermute(ready, axis_name='dp', perm=[(hop_no, hop_no ^ top) for hop_...]
    all_gather x1 -> x0, waiting for transfers between devices: 51.9 us -> none  [local(): mixer_full = lax.all_gather(gathered[0], 'dp', axis=1, tiled=True)]
    select_n x0 -> x3, other arithmetic: none -> 21.4 us  [close_wall_over_axis(): ready = jnp.where(prior & top == 0, a_next, current_block)]
    ppermute x6, waiting for transfers between devices: 68.6 us -> 55.4 us  [passed_along(): lax.ppermute(value, axis, [(source, source + steps) for source in range(l...]
    unnamed x11 -> x10, waiting for transfers between devices: 77.1 us -> 81.6 us
    unnamed x89 -> x97, local copies, waits for them, and re-layouts: 98 us -> 102 us
  transfers between devices with their start and end apart: 14 -> 16, of which waited for: 10 -> 12; matrix products, arithmetic and copies ran while one was open for 36% -> 31% of each run, Pallas kernels for 0% -> 0%
where the time goes in v1:
time: 1170 us; the launch traced here: 1160 us
  waiting for transfers between devices  529 us (45%)
  matrix products  338 us (29%)
  local copies, waits for them, and re-layouts  191 us (16%)
  other arithmetic  62.1 us (5%)
  starting transfers between devices  21.7 us (2%)
  between operations  15.2 us (1%)
    ppermute x3, waiting for transfers between devices, close_wall_over_axis(): lax.ppermute(ready, axis_name='dp', perm=[(hop_no, hop_no ^ top) for hop_...  233 us
    psum x1, waiting for transfers between devices, reduce_grads(): lax.psum(pieces[2].astype(jnp.bfloat16), 'seq').astype(jnp.float32)  104 us
    unnamed x97, local copies, waits for them, and re-layouts  102 us
    unnamed x10, waiting for transfers between devices  81.6 us
    reduce_scatter x1, waiting for transfers between devices, reduce_grads(): lax.psum_scatter(terms[3].astype(jnp.bfloat16), 'dp', scatter_dimension=0...  55.9 us
    ppermute x6, waiting for transfers between devices, passed_along(): lax.ppermute(value, axis, [(source, source + steps) for source in range(l...  55.4 us
    dot_general x1, matrix products, block_back(): jnp.einsum('rhts,rshd->rthd', score_grad, per_head_keys, precision=FULL_P...  28 us
    dot_general x1, matrix products, block_out(): jnp.einsum('rhts,rshe->rthe', scores, per_head_values, precision=FULL_PRE...  23.7 us
  transfers between devices with their start and end apart: 16, of which 12 were waited for; matrix products, arithmetic and copies ran while one was open for 31% of the time, Pallas kernels for 0%

profile of v1, /device:TPU:0, one launch (start us, length us, event | category | flops | bytes accessed | tf_op | source)
XLA Modules:
  0.0 1157.6 jit_solution(8983483292650208063)
XLA Ops:
  20.4 103.7 %collective-permute-done.3 = bf16[5,256,1024]{1,2,0:T(8,128)(2,1)} collective-permute-done((bf16[5,256,1024]{1,2,0:T(8,128)(2,1)}, bf16[5,256,1024]{1,2,0:T(8,128)(2,1)}, u32[]{:S(2)}, u32[]{:S(2)}) %collective-permute-start.3) | collective-permute-done | bytes 2621472 | tf_op jit(solution)/shard_map/ppermute | solution.py:14
  124.1 7.6 maximum_select_fusion.1
  142.7 126.2 %collective-permute-done.4 = bf16[5,512,1024]{1,2,0:T(8,128)(2,1)} collective-permute-done((bf16[5,512,1024]{1,2,0:T(8,128)(2,1)}, bf16[5,512,1024]{1,2,0:T(8,128)(2,1)}, u32[]{:S(2)}, u32[]{:S(2)}) %collective-permute-start.4) | collective-permute-done | bytes 5242912 | tf_op jit(solution)/shard_map/ppermute | solution.py:14
  268.9 11.9 %maximum_select_fusion = bf16[5,1024,1024]{1,2,0:T(8,128)(2,1)S(1)} fusion(bf16[5,512,1024]{1,2,0:T(8,128)(2,1)} %collective-permute-done.4, bf16[5,512,1024]{1,2,0:T(8,128)(2,1)} %maximum_select_fusion.1, pred[]{:T(512)S(6)} %eq.54), kind=kLoop, calls=%fused_computation.29 | loop fusion | flops 47185920 | bytes 20971520 | tf_op jit(solution)/shard_map/jit(_where)/select_n | solution.py:19
  284.7 11.7 %convolution_bitcast_fusion = f32[4,1024,1024]{1,2,0:T(8,128)} fusion(bf16[5,1024,1024]{1,2,0:T(8,128)(2,1)S(1)} %maximum_select_fusion, bf16[1024,1024]{1,0:T(8,128)(2,1)S(1)} %fusion.66), kind=kOutput, calls=%fused_computation.31 | convolution fusion | flops 8589934592 | bytes 29360128 | tf_op jit(solution)/shard_map/nd,kde->kne/dot_general | solution.py:212
  296.4 10.2 fusion.121
  313.1 7.2 copy.119
  326.9 6.8 squeeze.12
  333.7 8.6 fusion.70
  342.2 36.5 %while.22 = (s32[]{:T(128)}, f32[2,8,128,128]{3,2,1,0:T(8,128)S(1)}, f32[2,8,128,128]{3,2,1,0:T(8,128)S(1)}, f32[8]{0:T(128)S(1)}, pred[2]{0:T(512)(128)(4,1)S(1)}, /*index=5*/s32[]{:T(128)}, s32[]{:T(128)}) while((s32[]{:T(128)}, f32[2,8,128,128]{3,2,1,0:T(8,128)S(1)}, f32[2,8,128,128]{3,2,1,0:T(8,128)S(1)}, f32[8]{0:T(128)S(1)}, ...), condition=%wide.region_5.6_spmd.clone, body=%wide.region_4.5_spmd.clone.sunk | while | flops 1310739 | bytes 6291745 | solution.py:148
  346.0 8.6 collective-permute-done
  359.4 7.7 collective-permute-done
  371.9 6.8 collective-permute-done
  378.9 9.1 fusion.120
  388.0 17.3 %fusion.119 = f32[2,8,512,512]{3,2,1,0:T(8,128)} fusion(f32[2,512,8,128]{1,0,3,2:T(2,128)S(1)} %copy-done.14, f32[2,512,8,128]{1,0,3,2:T(2,128)S(1)} %copy-done.13), kind=kOutput, calls=%fused_computation.168 | convolution fusion | flops 6450839552 | bytes 25165824 | tf_op jit(solution)/shard_map/rthd,rshd->rhts/dot_general | solution.py:90
  405.3 23.7 %multiply_reduce_fusion.2 = (f32[2,512]{1,0:T(2,128)S(1)}, f32[2,512,8,128]{1,3,2,0:T(8,128)}) fusion(f32[2,512,8]{1,2,0:T(8,128)S(1)} %get-tuple-element.166, f32[2,8,128,512]{3,2,1,0:T(8,128)} %fusion.120, f32[2,512,8,128]{3,1,2,0:T(8,128)} %copy.119, f32[2,8,512,512]{3,2,1,0:T(8,128)} %fusion.119, f32[8,512,512]{2,1,0:T(8,128)} %multiply_exponential_fusion, ...), kind=kOutput, calls=%fused_computation.101 | convolution fusion | flops 6455032832 | bytes 38309888 | tf_op jit(solution)/shard_map/rhts,rshe->rthe/dot_general | solution.py:93
  429.0 7.5 copy.123
  448.6 7.6 multiply_reduce_fusion.1
  456.3 20.9 %fusion.19 = f32[2,1024,2816]{2,1,0:T(8,128)} fusion(bf16[1,2,1024,2816]{3,2,1,0:T(8,128)(2,1)} %all-gather.5.cloned.1.call-done, f32[1024,1024]{1,0:T(8,128)} %get-tuple-element.159, f32[1024]{0:T(1024)S(1)} %get-tuple-element.149), kind=kOutput, calls=%fused_computation.30 | convolution fusion | flops 11813257216 | bytes 38801408 | tf_op jit(solution)/shard_map/nd,kdf->knf/dot_general | solution.py:233
  477.2 14.9 %fusion.42 = (bf16[1,1024,2816]{2,1,0:T(8,128)(2,1)}, bf16[1,1024,2816]{2,1,0:T(8,128)(2,1)}) fusion(f32[2,1024,2816]{2,1,0:T(8,128)} %fusion.19, bf16[1024,1024]{1,0:T(8,128)(2,1)S(1)} %bitcast.231, bf16[1,2816,1024]{2,1,0:T(8,128)(2,1)} %all-gather.7.cloned.1.call-done), kind=kOutput, calls=%fused_computation.53 | convolution fusion | flops 5922881536 | bytes 42467328 | tf_op jit(solution)/shard_map/nd,fd->nf/dot_general | solution.py:299
  492.1 20.3 %fusion.63 = (f32[1024]{0:T(1024)S(1)}, f32[1024,1024,1]{1,0,2:T(8,128)}) fusion(f32[1024,1024]{1,0:T(8,128)} %get-tuple-element.159, bf16[1,2,1024,2816]{3,2,1,0:T(8,128)(2,1)} %all-gather.5.cloned.1.call-done, bf16[1,1024,2816]{2,1,0:T(8,128)(2,1)} %get-tuple-element.140, bf16[1,1024,2816]{2,1,0:T(8,128)(2,1)} %get-tuple-element.139), kind=kOutput, calls=%fused_computation.81 | convolution fusion | flops 11819023360 | bytes 31461376 | tf_op jit(solution)/shard_map/knf,kdf->nd/dot_general | solution.py:307
  517.1 7.2 multiply_reduce_fusion
  537.3 19.9 %fusion.8 = f32[2,8,128,512]{3,2,1,0:T(8,128)} fusion(f32[2,8,512,512]{3,2,1,0:T(8,128)} %fusion.119, f32[8,512,512]{2,1,0:T(8,128)} %multiply_exponential_fusion, pred[2,512,512]{2,1,0:T(8,128)(4,1)S(1)} %copy-done.17, f32[2,512,8,128]{1,0,3,2:T(2,128)} %reshape.344), kind=kOutput, calls=%fused_computation.12 | convolution fusion | flops 6450839552 | bytes 34078720 | tf_op jit(solution)/shard_map/rhts,rthe->rshe/dot_general | solution.py:133
  557.2 8.9 fusion.68
  566.1 16.0 %fusion.75 = f32[2,8,512,512]{3,2,1,0:T(8,128)} fusion(f32[2,512,8,128]{3,1,2,0:T(8,128)S(1)} %copy-done.5, f32[2,512,8,128]{1,0,3,2:T(2,128)S(1)} %copy-done.6), kind=kOutput, calls=%fused_computation.109 | convolution fusion | flops 6442450944 | bytes 25165824 | tf_op jit(solution)/shard_map/rthe,rshe->rhts/dot_general | solution.py:119
  588.0 39.9 %while.23 = (s32[]{:T(128)}, f32[2,8,128,128]{3,2,1,0:T(8,128)S(1)}, f32[2,8,128,128]{3,2,1,0:T(8,128)S(1)}, f32[8]{0:T(128)S(1)}, pred[2]{0:T(512)(128)(4,1)S(1)}, /*index=5*/s32[]{:T(128)}, s32[]{:T(128)}) while((s32[]{:T(128)}, f32[2,8,128,128]{3,2,1,0:T(8,128)S(1)}, f32[2,8,128,128]{3,2,1,0:T(8,128)S(1)}, f32[8]{0:T(128)S(1)}, ...), condition=%wide.region_11.12_spmd.clone, body=%wide.region_10.11_spmd.clone.sunk | while | flops 1310739 | bytes 6291745 | solution.py:157
  590.4 10.5 collective-permute-done.1
  603.4 11.4 collective-permute-done.1
  617.3 10.3 collective-permute-done.1
  628.0 8.1 fusion.124
  645.9 28.0 %fusion.11 = f32[2,8,128,512]{3,2,1,0:T(8,128)} fusion(f32[2,8,512,512]{3,2,1,0:T(8,128)} %fusion.75, f32[8,512,512]{2,1,0:T(8,128)} %multiply_exponential_fusion, pred[2,512,512]{2,1,0:T(8,128)(4,1)S(1)} %copy-done.17, f32[2,512,8,128]{1,0,3,2:T(2,128)} %squeeze.13), kind=kOutput, calls=%fused_computation.15 | convolution fusion | flops 6455033856 | bytes 34078720 | tf_op jit(solution)/shard_map/rhts,rshd->rthd/dot_general | solution.py:121
  673.9 8.5 fusion.59
  687.7 6.6 reshape.345
  694.3 21.6 %fusion.58 = f32[2,512,8,128]{1,3,2,0:T(8,128)} fusion(f32[2,8,128,512]{3,2,1,0:T(8,128)} %fusion.124, f32[2,8,512,512]{3,2,1,0:T(8,128)} %fusion.75, f32[8,512,512]{2,1,0:T(8,128)} %multiply_exponential_fusion, pred[2,512,512]{2,1,0:T(8,128)(4,1)S(1)} %copy-done.17, f32[2,512,8]{1,2,0:T(8,128)S(1)} %copy-done.32, f32[2,512,8,128]{1,0,3,2:T(2,128)} %squeeze.12), kind=kOutput, calls=%fused_computation.72 | convolution fusion | flops 6457131008 | bytes 38305792 | tf_op jit(solution)/shard_map/rhts,rthd->rshd/dot_general | solution.py:127
  715.9 7.5 copy.131
  730.1 8.0 multiply_convert_fusion.2
  740.1 11.0 convert_bitcast_fusion.1
  751.1 15.1 %copy.151 = bf16[4,1024,1024]{2,0,1:T(4,128)(2,1)} copy(bf16[4,1024,1024]{1,2,0:T(8,128)(2,1)} %convert_bitcast_fusion.1) | data formatting | bytes 16777216
  766.2 12.2 %copy.160 = bf16[128,8,4,1024]{3,1,2,0:T(8,128)(2,1)} copy(bf16[128,8,4,1024]{3,2,1,0:T(4,128)(2,1)} %bitcast.224) | data formatting | bytes 16777216
  778.5 19.5 %convert_bitcast_fusion = bf16[2,1024,2816]{1,2,0:T(8,128)(2,1)} fusion(bf16[1,1024,2816]{2,1,0:T(8,128)(2,1)} %get-tuple-element.140, bf16[1,1024,2816]{2,1,0:T(8,128)(2,1)} %get-tuple-element.139, f32[1024,1024]{1,0:T(8,128)} %get-tuple-element.159, f32[1024]{0:T(1024)S(1)} %get-tuple-element.149), kind=kOutput, calls=%fused_computation.28 | convolution fusion | flops 11824791552 | bytes 27267072 | tf_op jit(solution)/shard_map/nd,knf->kdf/dot_general | solution.py:304
  798.0 29.2 %copy.155 = bf16[2,1024,2816]{2,0,1:T(2,128)(2,1)} copy(bf16[2,1024,2816]{1,2,0:T(8,128)(2,1)} %convert_bitcast_fusion) | data formatting | bytes 23068672
  827.2 11.4 copy.161
  840.5 15.8 %fusion.46 = bf16[2816,1024]{1,0:T(8,128)(2,1)} fusion(bf16[1024,1024]{1,0:T(8,128)(2,1)S(1)} %bitcast.232, f32[2,1024,2816]{2,1,0:T(8,128)} %fusion.19), kind=kOutput, calls=%fused_computation.57 | convolution fusion | flops 5914230784 | bytes 30932992 | tf_op jit(solution)/shard_map/nf,nd->fd/dot_general | solution.py:297
  862.5 81.5 %reduce-scatter.17.cloned.1.call-done = bf16[128,5632]{1,0:T(8,128)(2,1)} async-done(((bf16[1024,5632]{1,0:T(8,128)(2,1)}), bf16[128,5632]{1,0:T(8,128)(2,1)}) %reduce-scatter.17.cloned.1.call-update) | async-done | bytes 1441808
  950.5 55.9 %reduce-scatter.11.cloned.1.call-done = bf16[352,1024]{1,0:T(8,128)(2,1)} async-done(((bf16[2816,1024]{1,0:T(8,128)(2,1)}), bf16[352,1024]{1,0:T(8,128)(2,1)}) %reduce-scatter.11.cloned.1.call-update) | async-done | bytes 720912 | tf_op jit(solution)/shard_map/reduce_scatter | solution.py:171
  1006.4 15.1 %fusion.55 = (f32[1024]{0:T(1024)S(1)}, f32[1024,1024,1]{1,0,2:T(8,128)S(1)}) fusion(bf16[2,512,1024]{2,1,0:T(8,128)(2,1)S(1)} %copy-done.12, bf16[5,1024,1024]{1,2,0:T(8,128)(2,1)} %copy-done.16, bf16[1,1024,1024]{1,2,0:T(8,128)(2,1)} %get-tuple-element.147, bf16[1,1024,1024]{1,2,0:T(8,128)(2,1)} %stack_reshape.4, bf16[1,1024,1024]{1,2,0:T(8,128)(2,1)} %copy-done.23, ...), kind=kOutput, calls=%fused_computation.67 | convolution fusion | flops 8605662208 | bytes 23072768 | tf_op jit(solution)/shard_map/kne,kde->nd/dot_general | solution.py:347
  1025.1 13.7 %add_convert_fusion = bf16[1024,1024]{1,0:T(8,128)(2,1)} fusion(f32[1024,1024]{1,0:T(8,128)S(1)} %copy-done.19, bf16[1,2816,1024]{2,1,0:T(8,128)(2,1)} %all-gather.7.cloned.1.call-done, f32[2,1024,2816]{2,1,0:T(8,128)} %fusion.19), kind=kOutput, calls=%fused_computation.97 | convolution fusion | flops 5913444352 | bytes 35127296 | tf_op jit(solution)/shard_map/dot_general | solution.py:31
  1038.8 103.7 %all-reduce.3.cloned.1.call-done = (bf16[1,2,128,2816]{2,3,1,0:T(8,128)(2,1)}, bf16[1,128,1024]{1,2,0:T(8,128)(2,1)}, bf16[4,128,1024]{1,2,0:T(8,128)(2,1)}, bf16[1,352,1024]{2,1,0:T(8,128)(2,1)}) async-done(((bf16[1,2,128,2816]{2,3,1,0:T(8,128)(2,1)}, bf16[1,128,1024]{1,2,0:T(8,128)(2,1)}, bf16[4,128,1024]{1,2,0:T(8,128)(2,1)}, bf16[1,352,1024]{2,1,0:T(8,128)(2,1)}), (bf16[1,2,128,2816]{2,3,1,0:T(8,128)(2,1)}, ...) | async-done | bytes 3473424 | tf_op jit(solution)/shard_map/psum | solution.py:178
  (183 shorter events, 147.1 us)
Async XLA Ops:
  7.2 449.1 %all-gather.5.cloned.1.call-start = ((), (), s32[]{:S(2)}) async-start(), calls=%async_computation.5 | async-start | bytes 12976128 | tf_op jit(solution)/shard_map/all_gather | solution.py:208
  10.3 466.9 %all-gather.7.cloned.1.call-start = ((), (), s32[]{:S(2)}) async-start(), calls=%async_computation.6 | async-start | bytes 6488064 | tf_op jit(solution)/shard_map/all_gather | solution.py:209
  12.4 3.2 collective-permute-start.2
  17.5 106.6 %collective-permute-start.3 = (bf16[5,256,1024]{1,2,0:T(8,128)(2,1)}, bf16[5,256,1024]{1,2,0:T(8,128)(2,1)}, u32[]{:S(2)}, u32[]{:S(2)}) collective-permute-start(bf16[5,256,1024]{1,2,0:T(8,128)(2,1)} %maximum_select_fusion.2), channel_id=1, source_target_pairs={{0,2},{1,3},{2,0},{3,1},{4,6},{5,7},{6,4},{7,5},{8,10},{9,11},{10,... | collective-permute-start | bytes 7864328 | tf_op jit(solution)/shard_map/ppermute | solution.py:14
  20.4 113.3 %copy-start.29 = (f32[1,352,1024]{2,1,0:T(8,128)S(1)}, f32[1,352,1024]{2,1,0:T(8,128)}, u32[]{:S(2)}) copy-start(f32[1,352,1024]{2,1,0:T(8,128)} %param.14) | copy-start | bytes 4325380
  20.4 114.3 %copy-start.10 = (bf16[2,512,1024]{2,1,0:T(8,128)(2,1)S(1)}, bf16[2,512,1024]{2,1,0:T(8,128)(2,1)}, u32[]{:S(2)}) copy-start(bf16[2,512,1024]{2,1,0:T(8,128)(2,1)} %param.11) | copy-start | bytes 6291460
  131.7 137.2 %collective-permute-start.4 = (bf16[5,512,1024]{1,2,0:T(8,128)(2,1)}, bf16[5,512,1024]{1,2,0:T(8,128)(2,1)}, u32[]{:S(2)}, u32[]{:S(2)}) collective-permute-start(bf16[5,512,1024]{1,2,0:T(8,128)(2,1)} %maximum_select_fusion.1), channel_id=1, source_target_pairs={{0,4},{1,5},{2,6},{3,7},{4,0},{5,1},{6,2},{7,3},{8,12},{9,13},{10,... | collective-permute-start | bytes 15728648 | tf_op jit(solution)/shard_map/ppermute | solution.py:14
  134.6 722.3 %reduce-scatter.15.cloned.1.call-start = ((), (), s32[]{:S(2)}) async-start(), calls=%async_computation.8 | async-start | bytes 2359296
  135.2 7.4 copy-start.33
  136.6 197.1 %copy-start.31 = (f32[2,512,8]{1,2,0:T(8,128)}, f32[2,512,8]{1,2,0:T(8,128)S(1)}, u32[]{:S(2)}) copy-start(f32[2,512,8]{1,2,0:T(8,128)S(1)} %get-tuple-element.167) | copy-start | bytes 98308
  138.2 142.5 %copy-start.24 = (bf16[1024,1024]{1,0:T(8,128)(2,1)}, bf16[1024,1024]{1,0:T(8,128)(2,1)S(1)}, u32[]{:S(2)}) copy-start(bf16[1024,1024]{1,0:T(8,128)(2,1)S(1)} %fusion.66) | copy-start | bytes 6291460
  342.5 12.0 %collective-permute-start = (bf16[2,8,128,128]{3,2,1,0:T(8,128)(2,1)S(1)}, bf16[2,8,128,128]{3,2,1,0:T(8,128)(2,1)S(1)}, u32[]{:S(2)}, u32[]{:S(2)}) collective-permute-start(bf16[2,8,128,128]{3,2,1,0:T(8,128)(2,1)S(1)} %fusion.138), channel_id=1, source_target_pairs={{0,8},{8,16},{16,24},{1,9},{9,17},{17,25},{2,10},{10,18},{18,26},{... | collective-permute-start | bytes 1572872 | tf_op jit(solution)/shard_map/while/body/eval_jaxpr/ppermute | solution.py:27
  355.0 12.1 %collective-permute-start = (bf16[2,8,128,128]{3,2,1,0:T(8,128)(2,1)S(1)}, bf16[2,8,128,128]{3,2,1,0:T(8,128)(2,1)S(1)}, u32[]{:S(2)}, u32[]{:S(2)}) collective-permute-start(bf16[2,8,128,128]{3,2,1,0:T(8,128)(2,1)S(1)} %fusion.138), channel_id=1, source_target_pairs={{0,8},{8,16},{16,24},{1,9},{9,17},{17,25},{2,10},{10,18},{18,26},{... | collective-permute-start | bytes 1572872 | tf_op jit(solution)/shard_map/while/body/eval_jaxpr/ppermute | solution.py:27
  367.5 11.2 collective-permute-start
  378.8 9.2 copy-start.8
  378.8 9.2 copy-start.35
  378.8 9.2 copy-start.37
  378.8 9.2 copy-start.13
  378.8 9.2 copy-start.14
  388.0 17.3 %copy-start.17 = (pred[2,512,512]{2,1,0:T(8,128)(4,1)S(1)}, pred[2,512,512]{2,1,0:T(8,128)(4,1)}, u32[]{:S(2)}) copy-start(pred[2,512,512]{2,1,0:T(8,128)(4,1)} %compare_and_fusion) | copy-start | bytes 1572868
  443.2 5.5 copy-start.11
  443.2 5.5 copy-start.18
  456.3 20.9 %copy-start.27 = (bf16[2,512,1024]{2,1,0:T(8,128)(2,1)S(1)}, bf16[2,512,1024]{2,1,0:T(8,128)(2,1)}, u32[]{:S(2)}) copy-start(bf16[2,512,1024]{2,1,0:T(8,128)(2,1)} %param.17) | copy-start | bytes 6291460
  517.1 7.2 copy-start.2
  557.2 8.9 copy-start.5
  557.2 8.9 copy-start.6
  566.0 16.0 %copy-start.1 = (f32[128,8,2,512]{3,1,2,0:T(8,128)S(1)}, f32[128,8,2,512]{3,1,2,0:T(8,128)}, u32[]{:S(2)}) copy-start(f32[128,8,2,512]{3,1,2,0:T(8,128)} %copy.159) | copy-start | bytes 12582916
  566.1 16.0 %copy-start.3 = (f32[1024,1024]{1,0:T(8,128)S(1)}, f32[1024,1024]{1,0:T(8,128)}, u32[]{:S(2)}) copy-start(f32[1024,1024]{1,0:T(8,128)} %copy-done.2) | copy-start | bytes 12582916
  582.1 6.0 copy-start.7
  582.1 6.0 copy-start.36
  582.1 6.0 copy-start.38
  589.1 11.8 %collective-permute-start.1 = (bf16[2,8,128,128]{3,2,1,0:T(8,128)(2,1)}, bf16[2,8,128,128]{3,2,1,0:T(8,128)(2,1)S(1)}, u32[]{:S(2)}, u32[]{:S(2)}) collective-permute-start(bf16[2,8,128,128]{3,2,1,0:T(8,128)(2,1)} %fusion.139), channel_id=1, source_target_pairs={{8,0},{16,8},{24,16},{9,1},{17,9},{25,17},{10,2},{18,10},{26,18},{... | collective-permute-start | bytes 1572872 | tf_op jit(solution)/shard_map/while/body/eval_jaxpr/ppermute | solution.py:27
  602.1 12.7 %collective-permute-start.1 = (bf16[2,8,128,128]{3,2,1,0:T(8,128)(2,1)}, bf16[2,8,128,128]{3,2,1,0:T(8,128)(2,1)S(1)}, u32[]{:S(2)}, u32[]{:S(2)}) collective-permute-start(bf16[2,8,128,128]{3,2,1,0:T(8,128)(2,1)} %fusion.139), channel_id=1, source_target_pairs={{8,0},{16,8},{24,16},{9,1},{17,9},{25,17},{10,2},{18,10},{26,18},{... | collective-permute-start | bytes 1572872 | tf_op jit(solution)/shard_map/while/body/eval_jaxpr/ppermute | solution.py:27
  616.0 11.6 %collective-permute-start.1 = (bf16[2,8,128,128]{3,2,1,0:T(8,128)(2,1)}, bf16[2,8,128,128]{3,2,1,0:T(8,128)(2,1)S(1)}, u32[]{:S(2)}, u32[]{:S(2)}) collective-permute-start(bf16[2,8,128,128]{3,2,1,0:T(8,128)(2,1)} %fusion.139), channel_id=1, source_target_pairs={{8,0},{16,8},{24,16},{9,1},{17,9},{25,17},{10,2},{18,10},{26,18},{... | collective-permute-start | bytes 1572872 | tf_op jit(solution)/shard_map/while/body/eval_jaxpr/ppermute | solution.py:27
  628.0 8.1 copy-start.15
  628.0 8.1 copy-start.20
  628.0 8.1 copy-start.32
  645.9 28.1 %copy-start.9 = (f32[2,8,128,128]{3,2,1,0:T(8,128)S(1)}, f32[2,8,128,128]{3,2,1,0:T(8,128)}, u32[]{:S(2)}) copy-start(f32[2,8,128,128]{3,2,1,0:T(8,128)} %copy-done.8) | copy-start | bytes 3145732
  730.0 10.1 copy-start.21
  730.0 128.7 %reduce-scatter.13.cloned.1.call-start = ((), (), s32[]{:S(2)}) async-start(), calls=%async_computation.7 | async-start | bytes 9437184
  730.1 10.0 copy-start.25
  730.1 10.0 copy-start.26
  778.4 165.6 %reduce-scatter.17.cloned.1.call-start = ((), (), s32[]{:S(2)}) async-start(), calls=%async_computation.9 | async-start | bytes 12976128
  838.6 167.7 %reduce-scatter.11.cloned.1.call-start = ((), (), s32[]{:S(2)}) async-start(), calls=%async_computation.4 | async-start | bytes 6488064 | tf_op jit(solution)/shard_map/reduce_scatter | solution.py:171
  856.3 286.1 %all-reduce.3.cloned.1.call-start = ((), (), s32[]{:S(2)}) async-start(), calls=%async_computation.10 | async-start | bytes 6946816 | tf_op jit(solution)/shard_map/psum | solution.py:178
  862.5 143.9 %copy-start.12 = (bf16[2,512,1024]{2,1,0:T(8,128)(2,1)S(1)}, bf16[2,512,1024]{2,1,0:T(8,128)(2,1)}, u32[]{:S(2)}) copy-start(bf16[2,512,1024]{2,1,0:T(8,128)(2,1)} %param.11) | copy-start | bytes 6291460
  1006.4 15.1 %copy-start.4 = (f32[1024,1024]{1,0:T(8,128)S(1)}, f32[1024,1024]{1,0:T(8,128)}, u32[]{:S(2)}) copy-start(f32[1024,1024]{1,0:T(8,128)} %copy-done.2) | copy-start | bytes 12582916
  1144.0 5.1 copy-start.30
  (9 other events, 26.2 us)
Sparse Core Ops, SparseCore 0:
  10.5 115.3 all-gather.4
  134.8 67.0 all-gather.6
  730.1 45.0 reduce-scatter.14
  778.9 74.8 reduce-scatter.12
  857.2 86.7 reduce-scatter.16
  947.3 59.0 reduce-scatter.10
  1009.8 132.6 all-reduce.2
